TPU v7x, 128 devices: a whole 4x4x4 slice. The times are simulated.
128 devices in a mesh: ctx: 8 (over z, x_hi), tp: 16 (over x_lo, y, core).
Axes of the slice: x: 4 (x_hi: 2, x_lo: 2; x = x_hi * 2 + x_lo), y: 4, z: 4, core: 2. Of those that a mesh axis runs over, the one named last changes fastest.
Arguments:
- residual_in: bfloat16 [1024, 8192], P('ctx', 'tp'), may hold values from -0.3 to 0.3
- dh_rest: bfloat16 [1024, 8192], P('ctx', 'tp'), may hold values from -0.29882812 to 0.29882812
- w_query: bfloat16 [8192, 8192], P(None, 'tp'), may hold values from -0.0625 to 0.0625
- w_key: bfloat16 [8192, 1024], P(None, 'tp'), may hold values from -0.0625 to 0.0625
- w_value: bfloat16 [8192, 1024], P(None, 'tp'), may hold values from -0.0625 to 0.0625
- q_raw: bfloat16 [1024, 8192], P('ctx', 'tp'), may hold values from -33 to 33
- k_raw: bfloat16 [1024, 1024], P('ctx'), may hold values from -33 to 33
- v_win: bfloat16 [1024, 1024], P('ctx'), may hold values from -6 to 6
- cache_k: bfloat16 [8192, 1024], P('ctx'), may hold values from -90 to 90
- cache_v: bfloat16 [8192, 1024], P('ctx'), may hold values from -6 to 6
- d_attn: bfloat16 [1024, 8192], P('ctx', 'tp'), may hold values from -6 to 6
- s_qk: float32 [128], replicated, may hold values from 0.8 to 5.5
- cache_live: int32 [1], replicated, may hold values from 4096 to 8192
Outputs:
- grad_input: float32 [1024, 8192], P('ctx', 'tp')
All inputs are finite; a program needn't handle non-finite values.
Results may differ from a plain program's by a relative error of at most 0.0025.
The roundings to bfloat16 on the way count: a program that leaves them out, or rounds other values in their place, can miss the bound.
Values may be sent and summed in bfloat16 or wider, within the bound.
No kernel may reach another device: no remote copies, remote signals or barrier semaphores. Data moves between devices by JAX's collectives and lax.ppermute only.
A program may use at most 128 MiB of HBM per device.

v0:
```python
import math
import jax
import jax.numpy as jnp
from jax import lax
from jax.sharding import PartitionSpec as P

D = 8192
KVH = 8
HD = 128
EPS = 1e-06


def swapped(block, axis, apart):
    count = lax.axis_size(axis)
    route = []
    for low in range(count):
        high = low | 1 << apart
        if high != low and high < count:
            route += [(low, high), (high, low)]
    return lax.ppermute(block, axis, route)


def unit_rows(values, qk_gain):
    width = values.shape[-1]
    mean_sq = jnp.mean(values * values, axis=-1, keepdims=True)
    return values * (lax.rsqrt(mean_sq + EPS) / math.sqrt(width)) * qk_gain


def unit_back(values, qk_gain, grad):
    width = values.shape[-1]
    mean_sq = jnp.mean(values * values, axis=-1, keepdims=True)
    factor = lax.rsqrt(mean_sq + EPS) / math.sqrt(width)
    weighted = qk_gain * grad
    inner = jnp.sum(weighted * values, axis=-1, keepdims=True)
    return factor * (weighted - values * inner / (width * (mean_sq + EPS)))


def contract_last(left, right):
    return lax.dot_general(
        left, right, (((1,), (1,)), ((), ())), preferred_element_type=jnp.float32
    )


def contract_first(left, right):
    return lax.dot_general(
        left, right, (((0,), (0,)), ((), ())), preferred_element_type=jnp.float32
    )


def on_device(
    residual_in,
    dh_rest,
    w_query,
    w_key,
    w_value,
    q_raw,
    k_raw,
    v_win,
    cache_k,
    cache_v,
    d_attn,
    s_qk,
    cache_live,
):
    tok_rows = q_raw.shape[0]
    ctx_count = lax.axis_size("ctx")
    tp_count = lax.axis_size("tp")
    head_count = q_raw.shape[1] // HD
    group_size = tp_count // KVH
    tp_index = lax.axis_index("tp")
    ctx_index = lax.axis_index("ctx")
    group_index = tp_index // group_size
    member = tp_index % group_size
    cache_rows = cache_k.shape[0]
    total_cache = cache_rows * ctx_count
    total_tokens = tok_rows * ctx_count
    score_scale = math.sqrt(HD)
    key_raw = lax.dynamic_slice_in_dim(k_raw, group_index * HD, HD, 1).astype(jnp.float32)
    window_pack = jnp.concatenate(
        [
            unit_rows(key_raw, s_qk).astype(jnp.bfloat16),
            lax.dynamic_slice_in_dim(v_win, group_index * HD, HD, 1),
        ],
        1,
    )
    raw_keys = lax.dynamic_slice(cache_k, (0, group_index * HD), (cache_rows, HD)).astype(
        jnp.float32
    )
    raw_values = lax.dynamic_slice(cache_v, (0, group_index * HD), (cache_rows, HD))
    all_cache = lax.all_gather(
        jnp.concatenate([unit_rows(raw_keys, s_qk).astype(jnp.bfloat16), raw_values], 1),
        "ctx",
        axis=0,
        tiled=True,
    )
    all_window = lax.all_gather(window_pack, "ctx", axis=0, tiled=True)
    query_raw = q_raw.astype(jnp.float32).reshape(tok_rows, head_count, HD)
    row_total = head_count * tok_rows
    query_rows = (
        unit_rows(query_raw, s_qk).astype(jnp.bfloat16).transpose(1, 0, 2).reshape(row_total, HD)
    )
    dout_rows = d_attn.reshape(tok_rows, head_count, HD).transpose(1, 0, 2).reshape(row_total, HD)
    query_pos = (
        total_cache + ctx_index * tok_rows + jnp.arange(row_total, dtype=jnp.int32) % tok_rows
    )
    floor_pos = total_cache - cache_live[0]
    all_keys = jnp.concatenate([all_cache, all_window], 0)
    block = math.gcd(math.gcd(1024, total_cache), total_tokens)
    key_blocks = all_keys[:, :HD].reshape(-1, block, HD)
    value_blocks = all_keys[:, HD:].reshape(-1, block, HD)
    block_starts = jnp.arange(key_blocks.shape[0], dtype=jnp.int32) * block
    cache_blocks = total_cache // block

    def block_scores(key_block, start):
        scores = contract_last(query_rows, key_block) * score_scale
        key_pos = start + jnp.arange(block, dtype=jnp.int32)
        visible = (key_pos[None, :] >= floor_pos) & (key_pos[None, :] <= query_pos[:, None])
        return (scores, visible)

    def stat_step(carry, inputs):
        row_max, row_sum, weighted = carry
        key_block, value_block, start = inputs
        scores, visible = block_scores(key_block, start)
        dprobs = contract_last(dout_rows, value_block)
        new_max = jnp.maximum(row_max, jnp.max(jnp.where(visible, scores, -1e30), axis=1))
        rescale = jnp.exp(row_max - new_max)
        expo = jnp.where(visible, jnp.exp(scores - new_max[:, None]), 0.0)
        row_sum = row_sum * rescale + jnp.sum(expo, axis=1)
        weighted = weighted * rescale + jnp.sum(expo * dprobs, axis=1)
        return ((new_max, row_sum, weighted), None)

    start_max = jnp.full((row_total,), -1e30, jnp.float32)
    start_zero = jnp.zeros((row_total,), jnp.float32)
    (row_max, row_sum, weighted), _ = lax.scan(
        stat_step, (start_max, start_zero, start_zero), (key_blocks, value_blocks, block_starts)
    )
    lse = row_max + jnp.log(row_sum)
    delta = weighted / row_sum

    def block_grads(key_block, value_block, start):
        scores, visible = block_scores(key_block, start)
        probs = jnp.where(visible, jnp.exp(scores - lse[:, None]), 0.0)
        dprobs = contract_last(dout_rows, value_block)
        dscores = (probs * (dprobs - delta[:, None])).astype(jnp.bfloat16)
        return (probs, dscores)

    def cache_step(dq_total, inputs):
        key_block, value_block, start = inputs
        probs, dscores = block_grads(key_block, value_block, start)
        return (
            dq_total
            + jnp.dot(dscores, key_block, preferred_element_type=jnp.float32) * score_scale,
            None,
        )

    def window_step(dq_total, inputs):
        key_block, value_block, start = inputs
        probs, dscores = block_grads(key_block, value_block, start)
        dq_total = (
            dq_total + jnp.dot(dscores, key_block, preferred_element_type=jnp.float32) * score_scale
        )
        key_grad = contract_first(dscores, query_rows) * score_scale
        value_grad = contract_first(probs.astype(jnp.bfloat16), dout_rows)
        return (dq_total, jnp.concatenate([key_grad, value_grad], 1))

    dq_rows = jnp.zeros((row_total, HD), jnp.float32)
    dq_rows, _ = lax.scan(
        cache_step,
        dq_rows,
        (key_blocks[:cache_blocks], value_blocks[:cache_blocks], block_starts[:cache_blocks]),
    )
    dq_rows, window_parts = lax.scan(
        window_step,
        dq_rows,
        (key_blocks[cache_blocks:], value_blocks[cache_blocks:], block_starts[cache_blocks:]),
    )
    window_grads = window_parts.reshape(total_tokens, 2 * HD)
    own_grads = lax.psum_scatter(window_grads, "ctx", scatter_dimension=0, tiled=True)
    own_grads = own_grads + swapped(own_grads, "tp", 0)
    key_cols = w_key.shape[1]
    grad_k_full = unit_back(key_raw, s_qk, own_grads[:, :HD]).astype(jnp.bfloat16)
    grad_v_full = own_grads[:, HD:].astype(jnp.bfloat16)
    grad_k = lax.dynamic_slice_in_dim(grad_k_full, member * key_cols, key_cols, 1)
    grad_v = lax.dynamic_slice_in_dim(grad_v_full, member * key_cols, key_cols, 1)
    dq_heads = dq_rows.reshape(head_count, tok_rows, HD).transpose(1, 0, 2)
    grad_q = (
        unit_back(query_raw, s_qk, dq_heads).astype(jnp.bfloat16).reshape(tok_rows, head_count * HD)
    )
    slab = lax.psum_scatter(
        contract_last(w_query, grad_q)
        + contract_last(w_key, grad_k)
        + contract_last(w_value, grad_v),
        "tp",
        scatter_dimension=0,
        tiled=True,
    )
    grad_total = slab.T + dh_rest.astype(jnp.float32)
    resid = residual_in.astype(jnp.float32)
    square_sum, inner_sum = lax.psum(
        (jnp.sum(resid * resid, axis=1), jnp.sum(grad_total * resid, axis=1)), "tp"
    )
    mean_sq = square_sum / D
    factor = lax.rsqrt(mean_sq + EPS) / math.sqrt(D)
    correction = inner_sum / (D * (mean_sq + EPS))
    return factor[:, None] * (grad_total - resid * correction[:, None])


def solution(mesh):
    return jax.shard_map(
        on_device,
        mesh=mesh,
        in_specs=(
            P("ctx", "tp"),
            P("ctx", "tp"),
            P(None, "tp"),
            P(None, "tp"),
            P(None, "tp"),
            P("ctx", "tp"),
            P("ctx", None),
            P("ctx", None),
            P("ctx", None),
            P("ctx", None),
            P("ctx", "tp"),
            P(),
            P(),
        ),
        out_specs=P("ctx", "tp"),
        check_vma=False,
    )
```

profile of v0, /device:TPU:1, one launch (start us, length us, event | category | flops | bytes accessed | tf_op | source)
XLA Modules:
  0.0 376.6 jit_solution(14605620880003129420)
XLA Ops:
  12.9 32.4 %all_gather.7 = bf16[1024,256]{0,1:T(8,128)(2,1)S(1)} all-gather(bf16[128,256]{0,1:T(8,128)(2,1)S(1)} %pad_maximum_fusion.3), channel_id=1, replica_groups=mesh['ctx'=8,'tp'=16] {'ctx'}, dimensions={0}, use_global_device_ids=true | all-gather | bytes 589824 | tf_op jit(solution)/shard_map/all_gather | solution.py:96
  53.2 34.4 %all-gather.2.cloned.1.call-done = bf16[8192,256]{1,0:T(8,128)(2,1)} async-done(((bf16[1024,256]{1,0:T(8,128)(2,1)}), bf16[8192,256]{1,0:T(8,128)(2,1)}) %all-gather.2.cloned.1.call-update) | async-done | bytes 4194320 | tf_op jit(solution)/shard_map/all_gather | solution.py:90
  87.6 7.5 %pad_maximum_fusion = (bf16[9216,128]{1,0:T(8,128)(2,1)}, bf16[9216,128]{1,0:T(8,128)(2,1)}) fusion(bf16[1024,256]{1,0:T(8,128)(2,1)S(1)} %copy.39, bf16[8192,256]{1,0:T(8,128)(2,1)} %all-gather.2.cloned.1.call-done), kind=kLoop, calls=%fused_computation.71 | loop fusion | flops 9437184 | bytes 9437184 | tf_op jit(solution)/shard_map/concatenate | solution.py:107
  95.1 84.7 %while.31 = (s32[]{:T(128)}, f32[512]{0:T(512)S(1)}, f32[512]{0:T(512)S(1)}, f32[512]{0:T(512)S(1)}, s32[9]{0:T(128)}, /*index=5*/s32[]{:T(128)}, bf16[9,1024,12...) while((s32[]{:T(128)}, f32[512]{0:T(512)S(1)}, ...), condition=%wide.region_9.10_spmd.clone, body=%wide.region_5.9_spmd.clone.sunk | while | flops 277882880 | bytes 15533248 | solution.py:134
  97.4 2.9 fusion.133
  106.8 2.9 fusion.133
  116.2 2.9 fusion.133
  125.6 2.9 fusion.133
  135.0 2.9 fusion.133
  144.5 2.9 fusion.133
  153.9 2.9 fusion.133
  163.3 2.9 fusion.133
  172.7 2.9 fusion.133
  183.6 4.5 %fusion.95 = (bf16[8192,128]{1,0:T(8,128)(2,1)}, bf16[8192,128]{1,0:T(8,128)(2,1)}) fusion(bf16[8192,256]{1,0:T(8,128)(2,1)} %all-gather.2.cloned.1.call-done), kind=kLoop, calls=%fused_computation.154 | loop fusion | bytes 8388608 | tf_op jit(solution)/shard_map/slice | solution.py:170
  188.1 72.3 %while.32 = (s32[]{:T(128)}, f32[512,128]{1,0:T(8,128)}, s32[8]{0:T(128)}, s32[]{:T(128)}, bf16[8,1024,128]{2,1,0:T(8,128)(2,1)}, /*index=5*/bf16[512,128]{1,0:T...) while((s32[]{:T(128)}, f32[512,128]{1,0:T(8,128)}, ...), condition=%wide.region_11.12_spmd.clone, body=%wide.region_10.11_spmd.clone.sunk | while | flops 407050752 | bytes 5787299 | solution.py:167
  193.4 3.7 fusion.144
  197.1 2.7 fusion.142
  202.3 3.8 %fusion.144 = f32[512,128]{1,0:T(8,128)} fusion(f32[1024,512]{1,0:T(8,128)} %fusion.142, bf16[512,128]{1,0:T(8,128)(2,1)S(1)} %get-tuple-element.522, f32[512]{0:T(512)} %get-tuple-element.523, f32[512]{0:T(512)} %get-tuple-element.520, s32[512]{0:T(512)S(1)} %fusion.143, s32[1024]{0:T(1024)S(1)} %iota_add_fusion.6, ...), kind=kOutput, calls=%fused_computation.37.clone.1 | convolution fusion | flops 272826368 | bytes 3289089 | tf_op jit(solution)/shard_map/while/body/eval_jaxpr/dot_general | solution.py:152
  206.2 2.7 fusion.142
  211.4 3.8 %fusion.144 = f32[512,128]{1,0:T(8,128)} fusion(f32[1024,512]{1,0:T(8,128)} %fusion.142, bf16[512,128]{1,0:T(8,128)(2,1)S(1)} %get-tuple-element.522, f32[512]{0:T(512)} %get-tuple-element.523, f32[512]{0:T(512)} %get-tuple-element.520, s32[512]{0:T(512)S(1)} %fusion.143, s32[1024]{0:T(1024)S(1)} %iota_add_fusion.6, ...), kind=kOutput, calls=%fused_computation.37.clone.1 | convolution fusion | flops 272826368 | bytes 3289089 | tf_op jit(solution)/shard_map/while/body/eval_jaxpr/dot_general | solution.py:152
  215.2 2.7 fusion.142
  220.5 3.8 fusion.144
  224.3 2.7 fusion.142
  229.5 3.8 fusion.144
  233.3 2.7 fusion.142
  238.6 3.8 %fusion.144 = f32[512,128]{1,0:T(8,128)} fusion(f32[1024,512]{1,0:T(8,128)} %fusion.142, bf16[512,128]{1,0:T(8,128)(2,1)S(1)} %get-tuple-element.522, f32[512]{0:T(512)} %get-tuple-element.523, f32[512]{0:T(512)} %get-tuple-element.520, s32[512]{0:T(512)S(1)} %fusion.143, s32[1024]{0:T(1024)S(1)} %iota_add_fusion.6, ...), kind=kOutput, calls=%fused_computation.37.clone.1 | convolution fusion | flops 272826368 | bytes 3289089 | tf_op jit(solution)/shard_map/while/body/eval_jaxpr/dot_general | solution.py:152
  247.6 3.8 %fusion.144 = f32[512,128]{1,0:T(8,128)} fusion(f32[1024,512]{1,0:T(8,128)} %fusion.142, bf16[512,128]{1,0:T(8,128)(2,1)S(1)} %get-tuple-element.522, f32[512]{0:T(512)} %get-tuple-element.523, f32[512]{0:T(512)} %get-tuple-element.520, s32[512]{0:T(512)S(1)} %fusion.143, s32[1024]{0:T(1024)S(1)} %iota_add_fusion.6, ...), kind=kOutput, calls=%fused_computation.37.clone.1 | convolution fusion | flops 272826368 | bytes 3289089 | tf_op jit(solution)/shard_map/while/body/eval_jaxpr/dot_general | solution.py:152
  251.4 2.7 fusion.142
  256.6 3.8 fusion.144
  265.3 6.3 %fusion.97 = f32[128,8192]{1,0:T(8,128)S(1)} fusion(bf16[128,512]{0,1:T(8,128)(2,1)S(1)} %bitcast.155, bf16[8192,512]{1,0:T(8,128)(2,1)} %param.19), kind=kOutput, calls=%fused_computation.156 | convolution fusion | flops 1073741824 | bytes 12713984 | tf_op jit(solution)/shard_map/dot_general | solution.py:39
  275.8 60.3 %reduce-scatter.5.cloned.1.call-done = f32[512,128]{0,1:T(8,128)} async-done(((f32[8192,128]{0,1:T(8,128)}), f32[512,128]{0,1:T(8,128)}) %reduce-scatter.5.cloned.1.call-update) | async-done | bytes 262160 | tf_op jit(solution)/shard_map/reduce_scatter | solution.py:189
  337.2 31.0 %all-reduce = (f32[128]{0:T(128)S(1)}, f32[128]{0:T(128)S(1)}) all-reduce(f32[128]{0:T(128)S(1)} %get-tuple-element.240, f32[128]{0:T(128)S(1)} %get-tuple-element.239), channel_id=1, replica_groups=mesh['ctx'=8,'tp'=16] {'tp'}, use_global_device_ids=true, to_apply=%region_17.18 | all-reduce | flops 256 | bytes 2048 | tf_op jit(solution)/shard_map/psum | solution.py:199
  (234 shorter events, 112.6 us)
Async XLA Ops:
  6.5 1.7 copy-start
  6.5 6.2 %copy-start.14 = (f32[128]{0:T(128)S(1)}, f32[128]{0:T(128)}, u32[]{:S(2)}) copy-start(f32[128]{0:T(128)} %param.28) | copy-start | bytes 1540
  6.5 81.1 %all-gather.2.cloned.1.call-start = ((), (), s32[]{:S(2)}) async-start(), calls=%async_computation.2 | async-start | bytes 4718592 | tf_op jit(solution)/shard_map/all_gather | solution.py:90
  8.3 37.2 %copy-start.12 = (bf16[128,512]{1,0:T(8,128)(2,1)S(1)}, bf16[128,512]{1,0:T(8,128)(2,1)}, u32[]{:S(2)}) copy-start(bf16[128,512]{1,0:T(8,128)(2,1)} %param.22) | copy-start | bytes 393220
  10.4 253.5 %reduce-scatter.3.cloned.1.call-start = ((), (), s32[]{:S(2)}) async-start(), calls=%async_computation.3 | async-start | bytes 1179648 | tf_op jit(solution)/shard_map/reduce_scatter | solution.py:178
  11.4 1.4 copy-start.6
  12.7 32.5 %copy-start.20 = (f32[128]{0:T(128)}, f32[128]{0:T(128)S(1)}, u32[]{:S(2)}) copy-start(f32[128]{0:T(128)S(1)} %get-tuple-element.304) | copy-start | bytes 1540
  45.3 134.5 %copy-start.2 = (bf16[1024,256]{0,1:T(8,128)(2,1)}, bf16[1024,256]{0,1:T(8,128)(2,1)S(1)}, u32[]{:S(2)}) copy-start(bf16[1024,256]{0,1:T(8,128)(2,1)S(1)} %all_gather.7) | copy-start | bytes 1572868
  95.1 84.7 %copy-start.16 = (s32[1024]{0:T(1024)S(1)}, s32[1024]{0:T(1024)}, u32[]{:S(2)}) copy-start(s32[1024]{0:T(1024)} %iota_add_fusion.2) | copy-start | bytes 12292
  95.1 84.7 %copy-start.19 = (s32[512]{0:T(512)S(1)}, s32[512]{0:T(512)}, u32[]{:S(2)}) copy-start(s32[512]{0:T(512)} %fusion.88) | copy-start | bytes 6148
  95.1 84.7 %copy-start.22 = (pred[1024]{0:T(1024)(128)(4,1)S(1)}, pred[1024]{0:T(1024)(128)(4,1)}, u32[]{:S(2)}) copy-start(pred[1024]{0:T(1024)(128)(4,1)} %broadcast_compare_fusion.2) | copy-start | bytes 3076
  100.3 2.3 copy-start.1
  109.7 2.3 copy-start.1
  119.1 2.3 copy-start.1
  128.5 2.3 copy-start.1
  137.9 2.3 copy-start.1
  147.3 2.3 copy-start.1
  156.7 2.3 copy-start.1
  166.2 2.3 copy-start.1
  175.6 2.3 copy-start.1
  183.6 152.6 %reduce-scatter.5.cloned.1.call-start = ((), (), s32[]{:S(2)}) async-start(), calls=%async_computation.4 | async-start | bytes 4456448 | tf_op jit(solution)/shard_map/reduce_scatter | solution.py:189
  260.4 3.3 copy-start.15
  260.4 3.3 copy-start.17
  263.9 7.7 %collective-permute-start = (f32[128,256]{0,1:T(8,128)}, f32[128,256]{0,1:T(8,128)S(1)}, u32[]{:S(2)}, u32[]{:S(2)}) collective-permute-start(f32[128,256]{0,1:T(8,128)} %reduce-scatter.3.cloned.1.call-done), channel_id=1, source_target_pairs={{0,1},{1,0},{2,3},{3,2},{4,5},{5,4},{6,7},{7,6},{8,9},{9,8},{10,11... | collective-permute-start | bytes 393224 | tf_op jit(solution)/shard_map/ppermute | solution.py:20
  265.3 6.4 %copy-start.11 = (f32[128,256]{0,1:T(8,128)S(1)}, f32[128,256]{0,1:T(8,128)}, u32[]{:S(2)}) copy-start(f32[128,256]{0,1:T(8,128)} %reduce-scatter.3.cloned.1.call-done) | copy-start | bytes 393220
  265.3 6.4 %copy-start.7 = (bf16[128,128]{0,1:T(8,128)(2,1)S(1)}, bf16[128,128]{0,1:T(8,128)(2,1)}, u32[]{:S(2)}) copy-start(bf16[128,128]{0,1:T(8,128)(2,1)} %copy-done.6) | copy-start | bytes 98308
  265.3 6.5 %copy-start.5 = (bf16[8192,64]{0,1:T(8,128)(2,1)S(1)}, bf16[8192,64]{0,1:T(8,128)(2,1)}, u32[]{:S(2)}) copy-start(bf16[8192,64]{0,1:T(8,128)(2,1)} %param.20) | copy-start | bytes 3145732
  265.3 6.5 %copy-start.10 = (f32[128,128]{0,1:T(8,128)S(1)}, f32[128,128]{0,1:T(8,128)}, u32[]{:S(2)}) copy-start(f32[128,128]{0,1:T(8,128)} %convert_element_type.44) | copy-start | bytes 196612
  265.3 6.5 %copy-start.21 = (f32[128]{0:T(128)S(1)}, f32[128]{0:T(128)}, u32[]{:S(2)}) copy-start(f32[128]{0:T(128)} %copy-done.20) | copy-start | bytes 1540
  265.3 6.5 %copy-start.23 = (f32[128]{0:T(128)S(1)}, f32[128]{0:T(128)}, u32[]{:S(2)}) copy-start(f32[128]{0:T(128)} %get-tuple-element.303) | copy-start | bytes 1540
  275.8 60.4 %copy-start.8 = (bf16[128,512]{1,0:T(8,128)(2,1)S(1)}, bf16[128,512]{1,0:T(8,128)(2,1)}, u32[]{:S(2)}) copy-start(bf16[128,512]{1,0:T(8,128)(2,1)} %param.17) | copy-start | bytes 393220
  275.8 60.4 %copy-start.9 = (bf16[128,512]{1,0:T(8,128)(2,1)S(1)}, bf16[128,512]{1,0:T(8,128)(2,1)}, u32[]{:S(2)}) copy-start(bf16[128,512]{1,0:T(8,128)(2,1)} %param.18) | copy-start | bytes 393220
  (4 other events, 4.7 us)
Sparse Core Ops, SparseCore 0:
  10.5 77.0 all-gather.1
  183.7 68.0 reduce-scatter.2
  275.9 60.1 reduce-scatter.4
where the time goes:
time: 379 us; the launch traced here: 377 us
  matrix products  108 us (28%)
  waiting for transfers between devices  94.8 us (25%)
  blocking collectives  63.5 us (17%)
  other arithmetic  62 us (16%)
  local copies, waits for them, and re-layouts  31.5 us (8%)
  between operations  14.2 us (4%)
    dot_general x31, matrix products, contract_last(): lax.dot_general(left, right, (((1,), (1,)), ((), ())), preferred_element_...  75.3 us
    reduce_scatter x1, waiting for transfers between devices, on_device(): lax.psum_scatter(contract_last(w_query, grad_q) + contract_last(w_key, gr...  60.3 us
    all_gather x1, waiting for transfers between devices, on_device(): lax.all_gather(jnp.concatenate([unit_rows(raw_keys, s_qk).astype(jnp.bflo...  34.4 us
    all_gather x1, blocking collectives, on_device(): all_window = lax.all_gather(window_pack, 'ctx', axis=0, tiled=True)  32.4 us
    psum x1, blocking collectives, on_device(): lax.psum((jnp.sum(resid * resid, axis=1), jnp.sum(grad_total * resid, axi...  31 us
    dot_general x8, matrix products, cache_step(): jnp.dot(dscores, key_block, preferred_element_type=jnp.float32)  30.1 us
    reduce_sum x9, other arithmetic, stat_step(): row_sum = row_sum * rescale + jnp.sum(expo, axis=1)  20.7 us
    add x18, other arithmetic, block_scores(): key_pos = start + jnp.arange(block, dtype=jnp.int32)  11.1 us
  transfers between devices with their start and end apart: 4, of which 2 were waited for; matrix products, arithmetic and copies ran while one was open for 25% of the time, Pallas kernels for 0%

commit v1 on v0

--- a/solution.py
+++ b/solution.py
@@ -87,11 +87,17 @@
         jnp.float32
     )
     raw_values = lax.dynamic_slice(cache_v, (0, group_index * HD), (cache_rows, HD))
-    all_cache = lax.all_gather(
-        jnp.concatenate([unit_rows(raw_keys, s_qk).astype(jnp.bfloat16), raw_values], 1),
-        "ctx",
+    all_cache = jnp.concatenate(
+        lax.all_to_all(
+            jnp.stack(
+                [jnp.concatenate([unit_rows(raw_keys, s_qk).astype(jnp.bfloat16), raw_values], 1)]
+                * lax.axis_size("ctx")
+            ),
+            "ctx",
+            0,
+            0,
+        ),
         axis=0,
-        tiled=True,
     )
     all_window = lax.all_gather(window_pack, "ctx", axis=0, tiled=True)
     query_raw = q_raw.astype(jnp.float32).reshape(tok_rows, head_count, HD)

time: 379 us -> 401 us (1.058)
  blocking collectives: 63.5 us -> 100 us
  waiting for transfers between devices: 94.8 us -> 59.7 us
  starting transfers between devices: 1.47 us -> 15 us
  local copies, waits for them, and re-layouts: 31.5 us -> 35.7 us
    all_gather x1, blocking collectives: 32.4 us -> 69 us  [on_device(): all_window = lax.all_gather(window_pack, 'ctx', axis=0, tiled=True)]
    all_gather x1 -> x0, waiting for transfers between devices: 34.4 us -> none  [on_device(): lax.all_gather(jnp.concatenate([unit_rows(raw_keys, s_qk).astype(jnp.bflo...]
    all_to_all x0 -> x1, starting transfers between devices: none -> 8.45 us  [on_device(): lax.all_to_all(jnp.stack([jnp.concatenate([unit_rows(raw_keys, s_qk).asty...]
    ppermute x1, starting transfers between devices: 1.39 us -> 6.44 us  [swapped(): return lax.ppermute(block, axis, route)]
  transfers between devices with their start and end apart: 4 -> 4, of which waited for: 2 -> 1; matrix products, arithmetic and copies ran while one was open for 25% -> 23% of each run, Pallas kernels for 0% -> 0%
where the time goes in v1:
time: 401 us; the launch traced here: 399 us
  matrix products  108 us (27%)
  blocking collectives  100 us (25%)
  other arithmetic  65 us (16%)
  waiting for transfers between devices  59.7 us (15%)
  local copies, waits for them, and re-layouts  35.7 us (9%)
  starting transfers between devices  15 us (4%)
  between operations  14.5 us (4%)
    dot_general x31, matrix products, contract_last(): lax.dot_general(left, right, (((1,), (1,)), ((), ())), preferred_element_...  75.1 us
    all_gather x1, blocking collectives, on_device(): all_window = lax.all_gather(window_pack, 'ctx', axis=0, tiled=True)  69 us
    reduce_scatter x1, waiting for transfers between devices, on_device(): lax.psum_scatter(contract_last(w_query, grad_q) + contract_last(w_key, gr...  59.6 us
    psum x1, blocking collectives, on_device(): lax.psum((jnp.sum(resid * resid, axis=1), jnp.sum(grad_total * resid, axi...  31 us
    dot_general x8, matrix products, cache_step(): jnp.dot(dscores, key_block, preferred_element_type=jnp.float32)  30.1 us
    reduce_sum x9, other arithmetic, stat_step(): row_sum = row_sum * rescale + jnp.sum(expo, axis=1)  20.7 us
    ge x18, other arithmetic, block_scores(): key_pos[None, :] >= floor_pos  12.9 us
    add x18, other arithmetic, block_scores(): key_pos = start + jnp.arange(block, dtype=jnp.int32)  12.9 us
  transfers between devices with their start and end apart: 4, of which 1 were waited for; matrix products, arithmetic and copies ran while one was open for 23% of the time, Pallas kernels for 0%

profile of v1, /device:TPU:1, one launch (start us, length us, event | category | flops | bytes accessed | tf_op | source)
XLA Modules:
  0.0 398.7 jit_solution(2435167038408281762)
XLA Ops:
  11.8 8.5 %all-to-all-start = ((bf16[8,1024,256]{2,1,0:T(8,128)(2,1)}), bf16[8,1024,256]{2,1,0:T(8,128)(2,1)}, u32[]{:S(2)}, u32[]{:S(2)}) async-start(bf16[8,1024,256]{2,1,0:T(8,128)(2,1)} %stack.2), calls=%async_computation | async-start | bytes 8388608 | tf_op jit(solution)/shard_map/all_to_all | solution.py:91
  22.8 69.0 %all_gather.3 = bf16[1024,256]{0,1:T(8,128)(2,1)S(1)} all-gather(bf16[128,256]{0,1:T(8,128)(2,1)S(1)} %pad_maximum_fusion.3), channel_id=1, replica_groups=mesh['ctx'=8,'tp'=16] {'ctx'}, dimensions={0}, use_global_device_ids=true | all-gather | bytes 589824 | tf_op jit(solution)/shard_map/all_gather | solution.py:102
  100.1 4.5 %fusion.95 = (bf16[8192,128]{1,0:T(8,128)(2,1)}, bf16[8192,128]{1,0:T(8,128)(2,1)}) fusion(bf16[8192,256]{1,0:T(8,128)(2,1)} %bitcast.2), kind=kLoop, calls=%fused_computation.154 | loop fusion | bytes 8388608 | tf_op jit(solution)/shard_map/slice | solution.py:176
  104.6 7.5 %pad_maximum_fusion = (bf16[9216,128]{1,0:T(8,128)(2,1)}, bf16[9216,128]{1,0:T(8,128)(2,1)}) fusion(bf16[1024,256]{1,0:T(8,128)(2,1)S(1)} %copy.39, bf16[8192,256]{1,0:T(8,128)(2,1)} %bitcast.2), kind=kLoop, calls=%fused_computation.71 | loop fusion | flops 9437184 | bytes 9437184 | tf_op jit(solution)/shard_map/concatenate | solution.py:113
  112.1 88.1 %while.31 = (s32[]{:T(128)}, f32[512]{0:T(512)S(1)}, f32[512]{0:T(512)S(1)}, f32[512]{0:T(512)S(1)}, s32[9]{0:T(128)}, /*index=5*/s32[]{:T(128)}, bf16[9,1024,12...) while((s32[]{:T(128)}, f32[512]{0:T(512)S(1)}, ...), condition=%wide.region_9.10_spmd.clone, body=%wide.region_5.9_spmd.clone.sunk | while | flops 277882880 | bytes 15533248 | solution.py:140
  114.9 2.9 fusion.133
  124.6 2.9 fusion.133
  134.4 2.9 fusion.133
  144.2 2.9 fusion.133
  154.0 2.9 fusion.133
  163.8 2.9 fusion.133
  173.6 2.9 fusion.133
  183.4 2.9 fusion.133
  193.2 2.9 fusion.133
  204.1 73.9 %while.32 = (s32[]{:T(128)}, f32[512,128]{1,0:T(8,128)}, s32[8]{0:T(128)}, s32[]{:T(128)}, bf16[8,1024,128]{2,1,0:T(8,128)(2,1)}, /*index=5*/bf16[512,128]{1,0:T...) while((s32[]{:T(128)}, f32[512,128]{1,0:T(8,128)}, ...), condition=%wide.region_11.12_spmd.clone, body=%wide.region_10.11_spmd.clone.sunk | while | flops 407050752 | bytes 5787299 | solution.py:173
  204.1 2.7 fusion.142
  209.6 3.7 fusion.144
  218.7 3.8 fusion.144
  222.5 2.7 fusion.142
  227.9 3.8 fusion.144
  231.7 2.7 fusion.142
  237.2 3.8 fusion.144
  246.4 3.8 fusion.144
  250.2 2.7 fusion.142
  255.7 3.8 fusion.144
  264.9 3.8 fusion.144
  268.7 2.7 fusion.142
  274.2 3.8 fusion.144
  281.4 6.4 %collective-permute-start = (f32[128,256]{0,1:T(8,128)}, f32[128,256]{0,1:T(8,128)S(1)}, u32[]{:S(2)}, u32[]{:S(2)}) collective-permute-start(f32[128,256]{0,1:T(8,128)} %reduce-scatter.3.cloned.1.call-done), channel_id=1, source_target_pairs={{0,1},{1,0},{2,3},{3,2},{4,5},{5,4},{6,7},{7,6},{8,9},{9,8},{10,11... | collective-permute-start | bytes 393224 | tf_op jit(solution)/shard_map/ppermute | solution.py:20
  287.9 6.3 %fusion.97 = f32[128,8192]{1,0:T(8,128)S(1)} fusion(bf16[128,512]{0,1:T(8,128)(2,1)S(1)} %bitcast.156, bf16[8192,512]{1,0:T(8,128)(2,1)} %param.19), kind=kOutput, calls=%fused_computation.156 | convolution fusion | flops 1073741824 | bytes 12713984 | tf_op jit(solution)/shard_map/dot_general | solution.py:39
  298.4 59.6 %reduce-scatter.5.cloned.1.call-done = f32[512,128]{0,1:T(8,128)} async-done(((f32[8192,128]{0,1:T(8,128)}), f32[512,128]{0,1:T(8,128)}) %reduce-scatter.5.cloned.1.call-update) | async-done | bytes 262160 | tf_op jit(solution)/shard_map/reduce_scatter | solution.py:195
  359.1 31.0 %all-reduce = (f32[128]{0:T(128)S(1)}, f32[128]{0:T(128)S(1)}) all-reduce(f32[128]{0:T(128)S(1)} %get-tuple-element.240, f32[128]{0:T(128)S(1)} %get-tuple-element.239), channel_id=1, replica_groups=mesh['ctx'=8,'tp'=16] {'tp'}, use_global_device_ids=true, to_apply=%region_17.18 | all-reduce | flops 256 | bytes 2048 | tf_op jit(solution)/shard_map/psum | solution.py:205
  (234 shorter events, 121.0 us)
Async XLA Ops:
  6.5 1.7 copy-start
  11.8 10.9 %copy-start.14 = (f32[128]{0:T(128)S(1)}, f32[128]{0:T(128)}, u32[]{:S(2)}) copy-start(f32[128]{0:T(128)} %param.28) | copy-start | bytes 1540
  11.8 88.3 %all-to-all-start = ((bf16[8,1024,256]{2,1,0:T(8,128)(2,1)}), bf16[8,1024,256]{2,1,0:T(8,128)(2,1)}, u32[]{:S(2)}, u32[]{:S(2)}) async-start(bf16[8,1024,256]{2,1,0:T(8,128)(2,1)} %stack.2), calls=%async_computation | async-start | bytes 8388608 | tf_op jit(solution)/shard_map/all_to_all | solution.py:91
  20.2 71.7 %copy-start.12 = (bf16[128,512]{1,0:T(8,128)(2,1)S(1)}, bf16[128,512]{1,0:T(8,128)(2,1)}, u32[]{:S(2)}) copy-start(bf16[128,512]{1,0:T(8,128)(2,1)} %param.22) | copy-start | bytes 393220
  20.2 261.2 %reduce-scatter.3.cloned.1.call-start = ((), (), s32[]{:S(2)}) async-start(), calls=%async_computation.3 | async-start | bytes 1179648 | tf_op jit(solution)/shard_map/reduce_scatter | solution.py:184
  21.3 1.5 copy-start.6
  22.7 69.1 %copy-start.20 = (f32[128]{0:T(128)}, f32[128]{0:T(128)S(1)}, u32[]{:S(2)}) copy-start(f32[128]{0:T(128)S(1)} %get-tuple-element.304) | copy-start | bytes 1540
  91.8 108.5 %copy-start.2 = (bf16[1024,256]{0,1:T(8,128)(2,1)}, bf16[1024,256]{0,1:T(8,128)(2,1)S(1)}, u32[]{:S(2)}) copy-start(bf16[1024,256]{0,1:T(8,128)(2,1)S(1)} %all_gather.3) | copy-start | bytes 1572868
  112.1 88.2 %copy-start.16 = (s32[1024]{0:T(1024)S(1)}, s32[1024]{0:T(1024)}, u32[]{:S(2)}) copy-start(s32[1024]{0:T(1024)} %iota_add_fusion.2) | copy-start | bytes 12292
  112.1 88.2 %copy-start.19 = (s32[512]{0:T(512)S(1)}, s32[512]{0:T(512)}, u32[]{:S(2)}) copy-start(s32[512]{0:T(512)} %fusion.88) | copy-start | bytes 6148
  112.1 88.2 %copy-start.22 = (pred[1024]{0:T(1024)(128)(4,1)S(1)}, pred[1024]{0:T(1024)(128)(4,1)}, u32[]{:S(2)}) copy-start(pred[1024]{0:T(1024)(128)(4,1)} %broadcast_compare_fusion.2) | copy-start | bytes 3076
  117.7 2.3 copy-start.1
  127.5 2.3 copy-start.1
  137.3 2.3 copy-start.1
  147.1 2.3 copy-start.1
  156.9 2.3 copy-start.1
  166.7 2.3 copy-start.1
  176.5 2.3 copy-start.1
  186.3 2.3 copy-start.1
  196.1 2.3 copy-start.1
  204.0 154.0 %reduce-scatter.5.cloned.1.call-start = ((), (), s32[]{:S(2)}) async-start(), calls=%async_computation.4 | async-start | bytes 4456448 | tf_op jit(solution)/shard_map/reduce_scatter | solution.py:195
  277.9 3.3 copy-start.15
  277.9 3.3 copy-start.17
  281.4 12.8 %collective-permute-start = (f32[128,256]{0,1:T(8,128)}, f32[128,256]{0,1:T(8,128)S(1)}, u32[]{:S(2)}, u32[]{:S(2)}) collective-permute-start(f32[128,256]{0,1:T(8,128)} %reduce-scatter.3.cloned.1.call-done), channel_id=1, source_target_pairs={{0,1},{1,0},{2,3},{3,2},{4,5},{5,4},{6,7},{7,6},{8,9},{9,8},{10,11... | collective-permute-start | bytes 393224 | tf_op jit(solution)/shard_map/ppermute | solution.py:20
  287.9 6.4 %copy-start.11 = (f32[128,256]{0,1:T(8,128)S(1)}, f32[128,256]{0,1:T(8,128)}, u32[]{:S(2)}) copy-start(f32[128,256]{0,1:T(8,128)} %reduce-scatter.3.cloned.1.call-done) | copy-start | bytes 393220
  287.9 6.4 %copy-start.7 = (bf16[128,128]{0,1:T(8,128)(2,1)S(1)}, bf16[128,128]{0,1:T(8,128)(2,1)}, u32[]{:S(2)}) copy-start(bf16[128,128]{0,1:T(8,128)(2,1)} %copy-done.6) | copy-start | bytes 98308
  287.9 6.5 %copy-start.5 = (bf16[8192,64]{0,1:T(8,128)(2,1)S(1)}, bf16[8192,64]{0,1:T(8,128)(2,1)}, u32[]{:S(2)}) copy-start(bf16[8192,64]{0,1:T(8,128)(2,1)} %param.20) | copy-start | bytes 3145732
  287.9 6.5 %copy-start.10 = (f32[128,128]{0,1:T(8,128)S(1)}, f32[128,128]{0,1:T(8,128)}, u32[]{:S(2)}) copy-start(f32[128,128]{0,1:T(8,128)} %convert_element_type.44) | copy-start | bytes 196612
  287.9 6.5 %copy-start.21 = (f32[128]{0:T(128)S(1)}, f32[128]{0:T(128)}, u32[]{:S(2)}) copy-start(f32[128]{0:T(128)} %copy-done.20) | copy-start | bytes 1540
  287.9 6.5 %copy-start.23 = (f32[128]{0:T(128)S(1)}, f32[128]{0:T(128)}, u32[]{:S(2)}) copy-start(f32[128]{0:T(128)} %get-tuple-element.303) | copy-start | bytes 1540
  298.3 59.6 %copy-start.8 = (bf16[128,512]{1,0:T(8,128)(2,1)S(1)}, bf16[128,512]{1,0:T(8,128)(2,1)}, u32[]{:S(2)}) copy-start(bf16[128,512]{1,0:T(8,128)(2,1)} %param.17) | copy-start | bytes 393220
  298.3 59.6 %copy-start.9 = (bf16[128,512]{1,0:T(8,128)(2,1)S(1)}, bf16[128,512]{1,0:T(8,128)(2,1)}, u32[]{:S(2)}) copy-start(bf16[128,512]{1,0:T(8,128)(2,1)} %param.18) | copy-start | bytes 393220
  (4 other events, 4.7 us)
Sparse Core Ops, SparseCore 0:
  204.1 72.4 reduce-scatter.2
  298.5 59.4 reduce-scatter.4
